TPU v7x, 128 devices: a whole 4x4x4 slice. The times are simulated.
128 devices in a mesh: node: 8 (over y_lo, z), bond: 16 (over y_hi, x, core).
Axes of the slice: x: 4, y: 4 (y_hi: 2, y_lo: 2; y = y_hi * 2 + y_lo), z: 4, core: 2. Of those that a mesh axis runs over, the one named last changes fastest.
Arguments:
- bottom_nodes: float32 [8, 128, 128, 128], P('node', 'bond'), may hold values from -0.046875 to 0.046875
- upper_nodes: float32 [8, 128, 128, 128], P(None, 'bond', 'node'), may hold values from -0.046875 to 0.046875
- leaf_up: float32 [8, 3, 2, 128, 128], P('node'), may hold values from -2 to 3
- outside_env: float32 [3, 128, 128], replicated, may hold values from -2 to 3
- top_env: float32 [3, 128, 128], replicated, may hold values from -2 to 3
Outputs:
- leaf_down: float32 [8, 3, 2, 128, 128], P('node', None, None, 'bond')
- subtree_env: float32 [3, 128, 128], replicated
All inputs are finite; a program needn't handle non-finite values.
Results may differ from a plain program's by a relative error of at most 0.0001.
Values sent between devices are 32-bit elements; how exact they have to be, the bound alone decides.
No kernel may reach another device: no remote copies, remote signals or barrier semaphores. Data moves between devices by JAX's collectives and lax.ppermute only.
A program may use at most 128 MiB of HBM per device.

v0:
```python
import jax
import jax.numpy as jnp
from jax import lax
from jax.sharding import Mesh, PartitionSpec as P

NODE = ("ylo", "zhi", "zlo")
BOND = ("yhi", "x", "core")
SLOT_OF = (4, 2, 5, 1, 6, 3, 7, 0)


def ein(spec, a, b):
    return jnp.einsum(spec, a, b, precision=lax.Precision.HIGHEST)


def after(x, other):
    return lax.optimization_barrier((x, other))[0]


def swap_cores(half, core, axis):
    other = lax.ppermute(half, "core", [(0, 1), (1, 0)])
    low = jnp.where(core == 0, half, other)
    high = jnp.where(core == 0, other, half)
    return jnp.concatenate([low, high], axis=axis)


def up_rows(tensor, rows, left_env, right_env):
    middle = ein("pab,ac->pcb", rows, left_env)
    product = ein("pcb,bd->pcd", middle, right_env)
    return ein("pcd,qcd->pq", product, tensor)


def halves(tensor, core, axis):
    size = tensor.shape[axis] // 2
    return lax.dynamic_slice_in_dim(tensor, core * size, size, axis=axis)


def local(bottom_nodes, upper_nodes, leaf_up, outside_env, top_env):
    group = lax.axis_index(NODE)
    bond = lax.axis_index(BOND)
    core = lax.axis_index("core")
    op = jnp.minimum(lax.axis_index("x"), 2)
    width = bottom_nodes.shape[2]
    rows = bottom_nodes.shape[1]
    parts = width // rows
    send = jnp.stack([upper_nodes[s] for s in SLOT_OF])
    got = lax.all_to_all(send, NODE, 0, 0, tiled=True)
    shard = jnp.moveaxis(got, 0, 1).reshape(rows, width, width)
    upper = lax.all_gather(shard, BOND, axis=0, tiled=True)
    mine = bottom_nodes[0]
    left_leaf = leaf_up[0, :, 0]
    right_leaf = leaf_up[0, :, 1]
    middle = ein("kac,pcd->kpad", left_leaf, after(mine, shard))
    product = ein("kpad,kbd->kpab", middle, right_leaf)
    both = jnp.concatenate([mine[None], product])
    both = jnp.moveaxis(both.reshape(4, rows, parts, rows, width), 2, 0)
    both = lax.all_to_all(both, BOND, 0, 0, tiled=True)
    both = jnp.moveaxis(both, 1, 0).reshape(4, width, rows, width)
    mine_a = both[0]
    gram = ein("pab,kqab->kpq", mine_a, both[1:])
    pieces = jnp.moveaxis(gram.reshape(3, parts, rows, width), 1, 0)
    pieces = lax.all_to_all(pieces, BOND, 0, 0, tiled=True)
    env = jnp.sum(pieces, axis=0)
    by_x = jnp.stack([env[0], env[1], env[2], env[2]])
    by_dest = jnp.broadcast_to(by_x[None, None, :, None], (2, 2, 4, 2, rows, width))
    by_dest = by_dest.reshape(2 * parts, rows, width)
    pair = lax.all_to_all(by_dest, ("zlo",) + BOND, 0, 0, tiled=True)
    left3, right3 = pair.reshape(2, width, width)

    def move(x, *pairs):
        return lax.ppermute(x, NODE, pairs)

    upper_rows = halves(upper, core, 0)
    up2 = up_rows(upper, upper_rows, left3, right3)
    ends = jnp.stack([move(up2, (0, 1), (4, 5)), move(up2, (2, 1), (6, 5))])
    left2, right2 = swap_cores(ends, core, 1)
    up1 = up_rows(upper, upper_rows, left2, right2)
    ends = jnp.stack([move(up1, (1, 3)), move(up1, (5, 3))])
    left1, right1 = swap_cores(ends, core, 1)
    upper_a = halves(upper, core, 1)
    upper_b = halves(upper, core, 2)

    def first_row(right_env):
        return ein("pab,bd->pad", upper_a, right_env)

    def second_row(left_env):
        return ein("pab,ac->pcb", upper_b, left_env)

    def worked_by(above):
        return ein("pq,qcd->pcd", above, upper)

    def first_of(row, worked):
        return ein("pad,pcd->ac", row, worked)

    def second_of(row, worked):
        return ein("pcb,pcd->bd", row, worked)

    top = lax.dynamic_index_in_dim(top_env, op, 0, keepdims=False)
    outside = lax.dynamic_index_in_dim(outside_env, op, 0, keepdims=False)
    crown = first_of(first_row(outside), worked_by(top))
    above = swap_cores(move(crown, (7, 3)), core, 0)
    worked = worked_by(above)
    first = first_of(first_row(right1), worked)
    second = second_of(second_row(left1), worked)
    root = up_rows(upper, upper_rows, left1, right1)
    above = swap_cores(move(first, (3, 1)) + move(second, (3, 5)), core, 0)
    worked = worked_by(above)
    first = first_of(first_row(right2), worked)
    second = second_of(second_row(left2), worked)
    above = move(first, (1, 0), (5, 4)) + move(second, (1, 2), (5, 6))
    above = swap_cores(above, core, 0)
    worked = worked_by(above)
    first = first_of(first_row(right3), worked)
    second = second_of(second_row(left3), worked)
    sent = move(second, (0, 1), (2, 3), (4, 5), (6, 7))
    last = jnp.where(group % 2 == 0, first, sent)
    root = jnp.where(group == 3, root, 0.0)
    root = root + move(root, (3, 7))
    root = root + move(root, (3, 1), (7, 5))
    root = root + move(root, (3, 2), (1, 0), (7, 6), (5, 4))
    ends = lax.all_gather(jnp.stack([last, root]), "x", axis=0, tiled=False)
    ends = swap_cores(ends[:3], core, 2)
    above = ends[:, 0]
    root_env = ends[:, 1]
    whole = lax.all_gather(after(mine, upper), BOND, axis=0, tiled=True)
    row = ein("pab,kbd->kpad", mine_a, right_leaf)
    grown = ein("kpq,kpad->kqad", above, row)
    first = ein("kqad,qcd->kac", grown, whole)
    turned = lax.dynamic_slice_in_dim(jnp.swapaxes(whole, 1, 2), bond * rows, rows, axis=1)
    row = ein("pba,kac->kbpc", turned, left_leaf)
    grown = ein("kpq,kbpc->kbqc", above, row)
    second = ein("kbqc,qcd->kbd", grown, whole)
    leaf_down = jnp.stack([first, second], 1)[None]
    return (leaf_down, root_env)


def solution(mesh):
    shape = (2, 2, 2, 2, 4, 2)
    fine = Mesh(mesh.devices.reshape(shape), NODE + BOND)
    placed = (
        P(NODE, BOND, None, None),
        P(None, BOND, NODE, None),
        P(NODE, None, None, None, None),
        P(),
        P(),
    )
    return jax.shard_map(
        local,
        mesh=fine,
        in_specs=placed,
        out_specs=(P(NODE, None, None, BOND, None), P()),
        check_vma=False,
    )
```

profile of v0, /device:TPU:67, one launch (start us, length us, event | category | flops | bytes accessed | tf_op | source)
XLA Modules:
  0.0 506.2 jit_solution(13400908433034332693)
XLA Ops:
  14.1 12.1 %all_to_all.20 = f32[8,8,16,128]{3,2,1,0:T(8,128)S(1)} all-to-all(f32[8,8,16,128]{3,2,1,0:T(8,128)S(1)} %slice_dynamic-update-slice_fusion), channel_id=1, replica_groups=mesh['ylo'=2,'zhi'=2,'zlo'=2,'yhi'=2,'x'=4,'core'=2] {'ylo','zhi','zlo'}, dimensions={0} | all-to-all | bytes 1048576 | tf_op jit(solution)/shard_map/all_to_all | solution.py:46
  31.7 40.8 %all_to_all.21 = f32[16,4,8,8,128]{4,3,2,1,0:T(8,128)S(1)} all-to-all(f32[16,4,8,8,128]{4,3,2,1,0:T(8,128)S(1)} %copy_bitcast_fusion.2), channel_id=1, replica_groups=mesh['ylo'=2,'zhi'=2,'zlo'=2,'yhi'=2,'x'=4,'core'=2] {'yhi','x','core'}, dimensions={0} | all-to-all | bytes 4194304 | tf_op jit(solution)/shard_map/all_to_all | solution.py:56
  81.1 7.2 %all-to-all-done.2 = f32[16,3,8,128]{3,2,1,0:T(8,128)S(1)} async-done(((f32[16,3,8,128]{3,2,1,0:T(8,128)}), f32[16,3,8,128]{3,2,1,0:T(8,128)S(1)}, u32[]{:S(2)}, u32[]{:S(2)}) %all-to-all-start.2) | async-done | bytes 196640 | tf_op jit(solution)/shard_map/all_to_all | solution.py:61
  94.4 36.1 %all-gather.4.cloned.1.call-done = f32[128,128,128]{2,0,1:T(8,128)} async-done(((f32[8,128,128]{2,0,1:T(8,128)}), f32[128,128,128]{2,0,1:T(8,128)}) %all-gather.4.cloned.1.call-update) | async-done | bytes 8388624 | tf_op jit(solution)/shard_map/all_gather | solution.py:48
  135.4 8.7 %fusion.26 = f32[128,64,128]{2,0,1:T(8,128)S(1)} fusion(f32[64,128,128]{2,0,1:T(8,128)} %constant_dynamic-slice_fusion.1, f32[32,8,128]{2,1,0:T(8,128)S(1)} %all-to-all-done.3), kind=kOutput, calls=%fused_computation.26 | convolution fusion | flops 1610612736 | bytes 8454144 | tf_op jit(solution)/shard_map/pab,ac->pcb/dot_general | solution.py:12
  144.1 6.3 %fusion.14 = f32[64,128,128]{2,0,1:T(8,128)S(1)} fusion(f32[128,64,128]{2,0,1:T(8,128)S(1)} %fusion.26, f32[32,8,128]{2,1,0:T(8,128)S(1)} %all-to-all-done.3), kind=kOutput, calls=%fused_computation.14 | convolution fusion | flops 1610612736 | bytes 8454144 | tf_op jit(solution)/shard_map/pcb,bd->pcd/dot_general | solution.py:12
  150.5 9.0 %convolution_bitcast_fusion.6 = f32[64,128]{1,0:T(8,128)S(1)} fusion(f32[64,128,128]{2,0,1:T(8,128)S(1)} %fusion.14, f32[128,128,128]{2,0,1:T(8,128)S(1)} %bitcast.242), kind=kOutput, calls=%fused_computation.59 | convolution fusion | flops 1610612736 | bytes 12615680 | tf_op jit(solution)/shard_map/pcd,qcd->pq/dot_general | solution.py:12
  175.3 9.4 %copy.46 = f32[128,128,128]{1,0,2:T(8,128)} copy(f32[128,128,128]{2,0,1:T(8,128)} %all-gather.4.cloned.1.call-done) | data formatting | bytes 16777216 | tf_op jit(solution)/shard_map/all_gather | solution.py:48
  184.7 10.9 %fusion.101 = f32[128,128,128]{1,0,2:T(8,128)S(1)} fusion(f32[128,128,128]{1,0,2:T(8,128)} %copy.46, f32[3,128,128]{2,1,0:T(8,128)S(1)} %copy-done, s32[]{:T(128)S(6)} %select_n.104), kind=kOutput, calls=%fused_computation.118 | convolution fusion | flops 3221225472 | bytes 16842756 | tf_op jit(solution)/shard_map/pq,qcd->pcd/dot_general | solution.py:12
  201.5 8.9 %constant_dynamic-slice_fusion = f32[128,128,64]{2,0,1:T(8,128)} fusion(f32[128,128,128]{2,0,1:T(8,128)} %all-gather.4.cloned.1.call-done, s32[]{:T(128)S(6)} %select_n.97), kind=kLoop, calls=%fused_computation.152 | loop fusion | bytes 8388612 | tf_op jit(solution)/shard_map/dynamic_slice | solution.py:34
  210.5 7.4 %copy.47 = f32[128,128,64]{0,1,2:T(8,128)} copy(f32[128,128,64]{2,0,1:T(8,128)} %constant_dynamic-slice_fusion) | data formatting | bytes 8388608 | tf_op jit(solution)/shard_map/dynamic_slice | solution.py:34
  219.3 11.8 %fusion.92 = f32[128,128,128]{2,0,1:T(8,128)} fusion(f32[128,128,128]{2,0,1:T(8,128)} %all-gather.4.cloned.1.call-done, f32[64,128]{1,0:T(8,128)S(1)} %get-tuple-element.21, f32[64,128]{1,0:T(8,128)S(1)} %get-tuple-element.20), kind=kOutput, calls=%fused_computation.106 | convolution fusion | flops 3221241856 | bytes 16842752 | tf_op jit(solution)/shard_map/pq,qcd->pcd/dot_general | solution.py:12
  231.1 9.4 %copy.27 = f32[128,128,128]{1,0,2:T(8,128)} copy(f32[128,128,128]{2,0,1:T(8,128)} %fusion.92) | data formatting | bytes 16777216 | tf_op jit(solution)/shard_map/pq,qcd->pcd/dot_general | solution.py:12
  240.5 8.8 %fusion.24 = f32[128,64,128]{2,0,1:T(8,128)S(1)} fusion(f32[64,128,128]{2,0,1:T(8,128)} %constant_dynamic-slice_fusion.1, f32[2,64,128]{2,1,0:T(8,128)S(1)} %get-tuple-element.15, f32[2,64,128]{2,1,0:T(8,128)S(1)} %get-tuple-element.14), kind=kOutput, calls=%fused_computation.24 | convolution fusion | flops 1610629120 | bytes 8519680 | tf_op jit(solution)/shard_map/pab,ac->pcb/dot_general | solution.py:12
  255.6 9.2 %convolution_bitcast_fusion.5 = f32[64,128]{1,0:T(8,128)S(1)} fusion(f32[64,128,128]{2,0,1:T(8,128)S(1)} %fusion.12, f32[128,128,128]{2,0,1:T(8,128)S(1)} %bitcast.244), kind=kOutput, calls=%fused_computation.58 | convolution fusion | flops 1610612736 | bytes 12615680 | tf_op jit(solution)/shard_map/pcd,qcd->pq/dot_general | solution.py:12
  287.7 11.0 %fusion.45 = f32[64,128]{1,0:T(8,128)S(1)} fusion(f32[128,128,128]{2,0,1:T(8,128)} %fusion.92, f32[128,128,64]{1,0,2:T(8,128)S(1)} %fusion.111), kind=kOutput, calls=%fused_computation.47 | convolution fusion | flops 1610612736 | bytes 12615680 | tf_op jit(solution)/shard_map/pcb,pcd->bd/dot_general | solution.py:12
  309.9 8.3 %convolution_bitcast_fusion.3 = f32[64,128]{1,0:T(8,128)S(1)} fusion(f32[128,64,128]{0,1,2:T(8,128)} %copy.44, f32[128,128,128]{1,0,2:T(8,128)} %copy.27), kind=kOutput, calls=%fused_computation.56 | convolution fusion | flops 1610612736 | bytes 12615680 | tf_op jit(solution)/shard_map/pad,pcd->ac/dot_general | solution.py:12
  325.0 6.9 %fusion.4 = f32[64,128,128]{2,0,1:T(8,128)S(1)} fusion(f32[128,64,128]{2,0,1:T(8,128)S(1)} %fusion.22, f32[2,64,128]{2,1,0:T(8,128)S(1)} %get-tuple-element.12, f32[2,64,128]{2,1,0:T(8,128)S(1)} %get-tuple-element.13), kind=kOutput, calls=%fused_computation.4 | convolution fusion | flops 1610629120 | bytes 8519680 | tf_op jit(solution)/shard_map/pcb,bd->pcd/dot_general | solution.py:12
  332.2 8.8 %fusion.54 = f32[64,128]{1,0:T(8,128)S(1)} fusion(f32[64,128,128]{2,0,1:T(8,128)S(1)} %fusion.4, f32[128,128,128]{2,0,1:T(8,128)S(1)} %bitcast.248, pred[]{:T(512)S(6)} %eq.9), kind=kOutput, calls=%fused_computation.51 | convolution fusion | flops 1610620928 | bytes 12615681 | tf_op jit(solution)/shard_map/pcd,qcd->pq/dot_general | solution.py:12
  342.5 9.5 %fusion.95 = f32[128,128,128]{2,0,1:T(8,128)} fusion(f32[128,128,128]{2,0,1:T(8,128)S(1)} %bitcast.248, f32[64,128]{1,0:T(8,128)S(1)} %get-tuple-element.19, f32[64,128]{1,0:T(8,128)S(1)} %get-tuple-element.18), kind=kOutput, calls=%fused_computation.110 | convolution fusion | flops 3221241856 | bytes 16842752 | tf_op jit(solution)/shard_map/pq,qcd->pcd/dot_general | solution.py:12
  352.0 9.4 %copy.28 = f32[128,128,128]{1,0,2:T(8,128)} copy(f32[128,128,128]{2,0,1:T(8,128)} %fusion.95) | data formatting | bytes 16777216 | tf_op jit(solution)/shard_map/pq,qcd->pcd/dot_general | solution.py:12
  361.4 10.7 %fusion.48 = f32[64,128]{1,0:T(8,128)S(1)} fusion(f32[128,128,128]{2,0,1:T(8,128)} %fusion.95, f32[128,128,64]{1,0,2:T(8,128)} %fusion.107), kind=kOutput, calls=%fused_computation.48 | convolution fusion | flops 1610612736 | bytes 12615680 | tf_op jit(solution)/shard_map/pcb,pcd->bd/dot_general | solution.py:12
  373.7 7.1 %convolution_bitcast_fusion.2 = f32[64,128]{1,0:T(8,128)S(1)} fusion(f32[128,64,128]{0,1,2:T(8,128)} %copy.42, f32[128,128,128]{1,0,2:T(8,128)S(1)} %copy-done.6), kind=kOutput, calls=%fused_computation.55 | convolution fusion | flops 1610612736 | bytes 12615680 | tf_op jit(solution)/shard_map/pad,pcd->ac/dot_general | solution.py:12
  399.7 10.5 %fusion.98 = f32[128,128,128]{2,0,1:T(8,128)S(1)} fusion(f32[128,128,128]{2,0,1:T(8,128)} %all-gather.4.cloned.1.call-done, f32[64,128]{1,0:T(8,128)S(1)} %get-tuple-element.17, f32[64,128]{1,0:T(8,128)S(1)} %get-tuple-element.16), kind=kOutput, calls=%fused_computation.114 | convolution fusion | flops 3221241856 | bytes 16842752 | tf_op jit(solution)/shard_map/pq,qcd->pcd/dot_general | solution.py:12
  410.2 7.4 %fusion.51 = f32[64,128]{1,0:T(8,128)S(1)} fusion(f32[128,128,128]{2,0,1:T(8,128)S(1)} %fusion.98, f32[128,128,64]{1,0,2:T(8,128)S(1)} %copy-done.7), kind=kOutput, calls=%fused_computation.49 | convolution fusion | flops 1610612736 | bytes 12615680 | tf_op jit(solution)/shard_map/pcb,pcd->bd/dot_general | solution.py:12
  417.6 9.0 %collective-permute-start.14 = (f32[64,128]{1,0:T(8,128)S(1)}, f32[64,128]{1,0:T(8,128)S(1)}, u32[]{:S(2)}, u32[]{:S(2)}) collective-permute-start(f32[64,128]{1,0:T(8,128)S(1)} %fusion.51), channel_id=1, source_target_pairs={{0,16},{32,48},{64,80},{96,112},{1,17},{33,49},{65,81},{97,113},{2... | collective-permute-start | bytes 98312 | tf_op jit(solution)/shard_map/ppermute | solution.py:70
  426.7 9.4 %copy.29 = f32[128,128,128]{1,0,2:T(8,128)} copy(f32[128,128,128]{2,0,1:T(8,128)} %copy-done.2) | data formatting | bytes 16777216 | tf_op jit(solution)/shard_map/pq,qcd->pcd/dot_general | solution.py:12
  436.1 8.2 %fusion.56 = f32[1,64,128]{2,1,0:T(8,128)S(1)} fusion(f32[64,128]{1,0:T(8,128)S(1)} %collective-permute-done.14, f32[128,64,128]{0,1,2:T(8,128)} %copy.39, f32[128,128,128]{1,0,2:T(8,128)} %copy.29, pred[]{:T(512)S(6)} %eq.8), kind=kOutput, calls=%fused_computation.54 | convolution fusion | flops 1610620928 | bytes 12648449 | tf_op jit(solution)/shard_map/pad,pcd->ac/dot_general | solution.py:12
  444.3 9.0 %all-gather = f32[8,64,128]{2,1,0:T(8,128)S(1)} all-gather(f32[2,64,128]{2,1,0:T(8,128)S(1)} %pad_maximum_fusion.5), channel_id=2, replica_groups=mesh['ylo'=2,'zhi'=2,'zlo'=2,'yhi'=2,'x'=4,'core'=2] {'x'}, dimensions={0}, use_global_device_ids=true | all-gather | bytes 327680 | tf_op jit(solution)/shard_map/all_gather | solution.py:120
  475.4 9.6 %copy.33 = f32[128,128,128]{2,0,1:T(8,128)} copy(f32[128,128,128]{1,0,2:T(8,128)} %all-gather.6.cloned.1.call-done) | data formatting | bytes 16777216 | tf_op jit(solution)/shard_map/all_gather | solution.py:124
  485.1 6.8 %fusion.60 = f32[3,1,8,128]{3,2,0,1:T(8,128)S(1)} fusion(f32[128,128,128]{2,0,1:T(8,128)} %copy.33, f32[3,8,128,128]{3,1,2,0:T(8,128)S(1)} %fusion.113), kind=kOutput, calls=%fused_computation.61 | convolution fusion | flops 603979776 | bytes 9973760 | tf_op jit(solution)/shard_map/kbqc,qcd->kbd/dot_general | solution.py:12
  491.9 6.7 %fusion.57 = f32[3,1,8,128]{3,2,0,1:T(8,128)S(1)} fusion(f32[3,128,8,128]{1,2,3,0:T(8,128)S(1)} %copy-done.12, f32[128,128,128]{1,0,2:T(8,128)} %all-gather.6.cloned.1.call-done), kind=kOutput, calls=%fused_computation.60 | convolution fusion | flops 603979776 | bytes 9973760 | tf_op jit(solution)/shard_map/kqad,qcd->kac/dot_general | solution.py:12
  (159 shorter events, 146.9 us)
Async XLA Ops:
  7.2 177.6 %copy-start = (f32[3,128,128]{2,1,0:T(8,128)S(1)}, f32[3,128,128]{2,1,0:T(8,128)}, u32[]{:S(2)}) copy-start(f32[3,128,128]{2,1,0:T(8,128)} %param.9) | copy-start | bytes 589828
  7.2 21.3 %copy-start.11 = (f32[1,3,2,128,128]{4,3,2,1,0:T(8,128)S(1)}, f32[1,3,2,128,128]{4,3,2,1,0:T(8,128)}, u32[]{:S(2)}) copy-start(f32[1,3,2,128,128]{4,3,2,1,0:T(8,128)} %param.7) | copy-start | bytes 1179652
  7.2 123.3 %all-gather.4.cloned.1.call-start = ((), (), s32[]{:S(2)}) async-start(), calls=%async_computation.4 | async-start | bytes 8912896 | tf_op jit(solution)/shard_map/all_gather | solution.py:48
  75.1 13.2 %all-to-all-start.2 = ((f32[16,3,8,128]{3,2,1,0:T(8,128)}), f32[16,3,8,128]{3,2,1,0:T(8,128)S(1)}, u32[]{:S(2)}, u32[]{:S(2)}) async-start(f32[16,3,8,128]{3,2,1,0:T(8,128)} %bitcast.240), calls=%async_computation.2 | async-start | bytes 393216 | tf_op jit(solution)/shard_map/all_to_all | solution.py:61
  89.1 46.3 %all-to-all-start.3 = ((f32[32,8,128]{2,1,0:T(8,128)}), f32[32,8,128]{2,1,0:T(8,128)S(1)}, u32[]{:S(2)}, u32[]{:S(2)}) async-start(f32[32,8,128]{2,1,0:T(8,128)} %bitcast.22), calls=%async_computation.3 | async-start | bytes 262144 | tf_op jit(solution)/shard_map/all_to_all | solution.py:66
  94.3 372.3 %all-gather.6.cloned.1.call-start = ((), (), s32[]{:S(2)}) async-start(), calls=%async_computation.5 | async-start | bytes 8912896 | tf_op jit(solution)/shard_map/all_gather | solution.py:124
  135.4 15.1 %slice-start = ((s8[8388608]{0:T(1024)(128)(4,1)}), s8[4194304]{0:T(1024)(128)(4,1)S(1)}, s32[]{:S(2)}) async-start(s8[8388608]{0:T(1024)(128)(4,1)} %bitcast.241), calls=%async_computation.6 | async-start | bytes 8388608
  159.5 59.0 %collective-permute-start = (f32[64,128]{1,0:T(8,128)S(1)}, f32[64,128]{1,0:T(8,128)S(1)}, u32[]{:S(2)}, u32[]{:S(2)}) collective-permute-start(f32[64,128]{1,0:T(8,128)S(1)} %convolution_bitcast_fusion.6), channel_id=1, source_target_pairs={{0,16},{64,80},{1,17},{65,81},{2,18},{66,82},{3,19},{67,83},{4,20}... | collective-permute-start | bytes 98312 | tf_op jit(solution)/shard_map/ppermute | solution.py:70
  160.1 58.3 %collective-permute-start.1 = (f32[64,128]{1,0:T(8,128)S(1)}, f32[64,128]{1,0:T(8,128)S(1)}, u32[]{:S(2)}, u32[]{:S(2)}) collective-permute-start(f32[64,128]{1,0:T(8,128)S(1)} %convolution_bitcast_fusion.6), channel_id=1, source_target_pairs={{32,16},{96,80},{33,17},{97,81},{34,18},{98,82},{35,19},{99,83},{3... | collective-permute-start | bytes 98312 | tf_op jit(solution)/shard_map/ppermute | solution.py:70
  200.9 17.0 %collective-permute-start.6 = (f32[64,128]{1,0:T(8,128)S(1)}, f32[64,128]{1,0:T(8,128)S(1)}, u32[]{:S(2)}, u32[]{:S(2)}) collective-permute-start(f32[64,128]{1,0:T(8,128)S(1)} %convolution_bitcast_fusion.4), channel_id=1, source_target_pairs={{112,48},{113,49},{114,50},{115,51},{116,52},{117,53},{118,54},{11... | collective-permute-start | bytes 98312 | tf_op jit(solution)/shard_map/ppermute | solution.py:70
  217.8 1.4 collective-permute-start.7
  218.4 22.0 %collective-permute-start.2 = (f32[2,64,128]{2,1,0:T(8,128)S(1)}, f32[2,64,128]{2,1,0:T(8,128)S(1)}, u32[]{:S(2)}, u32[]{:S(2)}) collective-permute-start(f32[2,64,128]{2,1,0:T(8,128)S(1)} %pad_maximum_fusion.3), channel_id=1, source_target_pairs={{0,1},{1,0},{2,3},{3,2},{4,5},{5,4},{6,7},{7,6},{8,9},{9,8},{10,11... | collective-permute-start | bytes 196616 | tf_op jit(solution)/shard_map/ppermute | solution.py:20
  240.5 15.1 %slice-start.2 = ((s8[8388608]{0:T(1024)(128)(4,1)}), s8[4194304]{0:T(1024)(128)(4,1)S(1)}, s32[]{:S(2)}) async-start(s8[8388608]{0:T(1024)(128)(4,1)} %bitcast.243), calls=%async_computation.8 | async-start | bytes 8388608
  264.9 6.5 %collective-permute-start.3 = (f32[64,128]{1,0:T(8,128)S(1)}, f32[64,128]{1,0:T(8,128)S(1)}, u32[]{:S(2)}, u32[]{:S(2)}) collective-permute-start(f32[64,128]{1,0:T(8,128)S(1)} %convolution_bitcast_fusion.5), channel_id=1, source_target_pairs={{16,48},{17,49},{18,50},{19,51},{20,52},{21,53},{22,54},{23,55},{2... | collective-permute-start | bytes 98312 | tf_op jit(solution)/shard_map/ppermute | solution.py:70
  265.5 5.8 %collective-permute-start.4 = (f32[64,128]{1,0:T(8,128)S(1)}, f32[64,128]{1,0:T(8,128)S(1)}, u32[]{:S(2)}, u32[]{:S(2)}) collective-permute-start(f32[64,128]{1,0:T(8,128)S(1)} %convolution_bitcast_fusion.5), channel_id=1, source_target_pairs={{80,48},{81,49},{82,50},{83,51},{84,52},{85,53},{86,54},{87,55},{8... | collective-permute-start | bytes 98312 | tf_op jit(solution)/shard_map/ppermute | solution.py:70
  271.4 10.7 %collective-permute-start.5 = (f32[2,64,128]{2,1,0:T(8,128)S(1)}, f32[2,64,128]{2,1,0:T(8,128)S(1)}, u32[]{:S(2)}, u32[]{:S(2)}) collective-permute-start(f32[2,64,128]{2,1,0:T(8,128)S(1)} %pad_maximum_fusion.4), channel_id=1, source_target_pairs={{0,1},{1,0},{2,3},{3,2},{4,5},{5,4},{6,7},{7,6},{8,9},{9,8},{10,11... | collective-permute-start | bytes 196616 | tf_op jit(solution)/shard_map/ppermute | solution.py:20
  282.1 17.3 %slice-start.4 = ((s8[8388608]{0:T(1024)(128)(4,1)}), s8[4194304]{0:T(1024)(128)(4,1)S(1)}, s32[]{:S(2)}) async-start(s8[8388608]{0:T(1024)(128)(4,1)} %bitcast.245), calls=%async_computation.10 | async-start | bytes 8388608
  298.7 33.2 %collective-permute-start.9 = (f32[64,128]{1,0:T(8,128)S(1)}, f32[64,128]{1,0:T(8,128)S(1)}, u32[]{:S(2)}, u32[]{:S(2)}) collective-permute-start(f32[64,128]{1,0:T(8,128)S(1)} %fusion.45), channel_id=1, source_target_pairs={{48,80},{49,81},{50,82},{51,83},{52,84},{53,85},{54,86},{55,87},{5... | collective-permute-start | bytes 98312 | tf_op jit(solution)/shard_map/ppermute | solution.py:70
  318.2 13.8 %collective-permute-start.8 = (f32[64,128]{1,0:T(8,128)S(1)}, f32[64,128]{1,0:T(8,128)S(1)}, u32[]{:S(2)}, u32[]{:S(2)}) collective-permute-start(f32[64,128]{1,0:T(8,128)S(1)} %convolution_bitcast_fusion.3), channel_id=1, source_target_pairs={{48,16},{49,17},{50,18},{51,19},{52,20},{53,21},{54,22},{55,23},{5... | collective-permute-start | bytes 98312 | tf_op jit(solution)/shard_map/ppermute | solution.py:70
  318.9 13.4 %slice-start.6 = ((s8[8388608]{0:T(1024)(128)(4,1)}), s8[4194304]{0:T(1024)(128)(4,1)S(1)}, s32[]{:S(2)}) async-start(s8[8388608]{0:T(1024)(128)(4,1)} %bitcast.247), calls=%async_computation.12 | async-start | bytes 8388608
  332.0 10.5 %collective-permute-start.10 = (f32[64,128]{1,0:T(8,128)S(1)}, f32[64,128]{1,0:T(8,128)S(1)}, u32[]{:S(2)}, u32[]{:S(2)}) collective-permute-start(f32[64,128]{1,0:T(8,128)S(1)} %add.49), channel_id=1, source_target_pairs={{0,1},{1,0},{2,3},{3,2},{4,5},{5,4},{6,7},{7,6},{8,9},{9,8},{10,11... | collective-permute-start | bytes 98312 | tf_op jit(solution)/shard_map/ppermute | solution.py:20
  341.0 45.6 %collective-permute-start.15 = (f32[64,128]{1,0:T(8,128)S(1)}, f32[64,128]{1,0:T(8,128)S(1)}, u32[]{:S(2)}, u32[]{:S(2)}) collective-permute-start(f32[64,128]{1,0:T(8,128)S(1)} %fusion.54), channel_id=1, source_target_pairs={{48,112},{49,113},{50,114},{51,115},{52,116},{53,117},{54,118},{55... | collective-permute-start | bytes 98312 | tf_op jit(solution)/shard_map/ppermute | solution.py:70
  361.4 26.2 %slice-start.8 = ((s8[8388608]{0:T(1024)(128)(4,1)}), s8[4194304]{0:T(1024)(128)(4,1)S(1)}, s32[]{:S(2)}) async-start(s8[8388608]{0:T(1024)(128)(4,1)} %bitcast.249), calls=%async_computation.14 | async-start | bytes 8388608
  372.1 15.5 %slice-start.9 = ((s8[8388608]{0:T(1024)(128)(4,1)}), s8[4194304]{0:T(1024)(128)(4,1)S(1)}, s32[]{:S(2)}) async-start(s8[8388608]{0:T(1024)(128)(4,1)} %bitcast.249), calls=%async_computation.15 | async-start | bytes 8388608
  372.1 15.2 %collective-permute-start.12 = (f32[64,128]{1,0:T(8,128)S(1)}, f32[64,128]{1,0:T(8,128)S(1)}, u32[]{:S(2)}, u32[]{:S(2)}) collective-permute-start(f32[64,128]{1,0:T(8,128)S(1)} %fusion.48), channel_id=1, source_target_pairs={{16,32},{80,96},{17,33},{81,97},{18,34},{82,98},{19,35},{83,99},{2... | collective-permute-start | bytes 98312 | tf_op jit(solution)/shard_map/ppermute | solution.py:70
  380.8 6.6 %collective-permute-start.11 = (f32[64,128]{1,0:T(8,128)S(1)}, f32[64,128]{1,0:T(8,128)S(1)}, u32[]{:S(2)}, u32[]{:S(2)}) collective-permute-start(f32[64,128]{1,0:T(8,128)S(1)} %convolution_bitcast_fusion.2), channel_id=1, source_target_pairs={{16,0},{80,64},{17,1},{81,65},{18,2},{82,66},{19,3},{83,67},{20,4}... | collective-permute-start | bytes 98312 | tf_op jit(solution)/shard_map/ppermute | solution.py:70
  386.7 11.3 %collective-permute-start.16 = (f32[64,128]{1,0:T(8,128)S(1)}, f32[64,128]{1,0:T(8,128)S(1)}, u32[]{:S(2)}, u32[]{:S(2)}) collective-permute-start(f32[64,128]{1,0:T(8,128)S(1)} %add.51), channel_id=1, source_target_pairs={{48,16},{112,80},{49,17},{113,81},{50,18},{114,82},{51,19},{115,83... | collective-permute-start | bytes 98312 | tf_op jit(solution)/shard_map/ppermute | solution.py:70
  387.4 12.3 %collective-permute-start.13 = (f32[64,128]{1,0:T(8,128)S(1)}, f32[64,128]{1,0:T(8,128)S(1)}, u32[]{:S(2)}, u32[]{:S(2)}) collective-permute-start(f32[64,128]{1,0:T(8,128)S(1)} %add.50), channel_id=1, source_target_pairs={{0,1},{1,0},{2,3},{3,2},{4,5},{5,4},{6,7},{7,6},{8,9},{9,8},{10,11... | collective-permute-start | bytes 98312 | tf_op jit(solution)/shard_map/ppermute | solution.py:20
  397.9 28.7 %collective-permute-start.17 = (f32[64,128]{1,0:T(8,128)S(1)}, f32[64,128]{1,0:T(8,128)S(1)}, u32[]{:S(2)}, u32[]{:S(2)}) collective-permute-start(f32[64,128]{1,0:T(8,128)S(1)} %add.52), channel_id=1, source_target_pairs={{48,32},{16,0},{112,96},{80,64},{49,33},{17,1},{113,97},{81,65},{5... | collective-permute-start | bytes 98312 | tf_op jit(solution)/shard_map/ppermute | solution.py:70
  417.6 18.5 %collective-permute-start.14 = (f32[64,128]{1,0:T(8,128)S(1)}, f32[64,128]{1,0:T(8,128)S(1)}, u32[]{:S(2)}, u32[]{:S(2)}) collective-permute-start(f32[64,128]{1,0:T(8,128)S(1)} %fusion.51), channel_id=1, source_target_pairs={{0,16},{32,48},{64,80},{96,112},{1,17},{33,49},{65,81},{97,113},{2... | collective-permute-start | bytes 98312 | tf_op jit(solution)/shard_map/ppermute | solution.py:70
  453.3 8.6 %collective-permute-start.18 = (f32[3,2,64,128]{3,2,0,1:T(8,128)S(1)}, f32[3,2,64,128]{3,2,0,1:T(8,128)S(1)}, u32[]{:S(2)}, u32[]{:S(2)}) collective-permute-start(f32[3,2,64,128]{3,2,0,1:T(8,128)S(1)} %copy.31), channel_id=1, source_target_pairs={{0,1},{1,0},{2,3},{3,2},{4,5},{5,4},{6,7},{7,6},{8,9},{9,8},{10,11... | collective-permute-start | bytes 589832 | tf_op jit(solution)/shard_map/ppermute | solution.py:20
  485.1 14.1 %copy-start.1 = (f32[3,128,128]{2,1,0:T(8,128)S(1)}, f32[3,128,128]{2,1,0:T(8,128)}, u32[]{:S(2)}) copy-start(f32[3,128,128]{2,1,0:T(8,128)} %param.9) | copy-start | bytes 589828
  (14 other events, 116.9 us)
Sparse Core Ops, SparseCore 0:
  27.3 103.1 all-gather.3
  132.7 76.9 all-gather.5
where the time goes:
time: 516 us; the launch traced here: 506 us
  matrix products  236 us (46%)
  local copies, waits for them, and re-layouts  108 us (21%)
  blocking collectives  61.9 us (12%)
  waiting for transfers between devices  44.2 us (9%)
  starting transfers between devices  39.6 us (8%)
  between operations  15.1 us (3%)
    dot_general x36, matrix products, ein(): return jnp.einsum(spec, a, b, precision=lax.Precision.HIGHEST)  236 us
    dot_general x9, local copies, waits for them, and re-layouts, ein(): return jnp.einsum(spec, a, b, precision=lax.Precision.HIGHEST)  52 us
    all_to_all x1, blocking collectives, local(): both = lax.all_to_all(both, BOND, 0, 0, tiled=True)  40.8 us
    all_gather x1, waiting for transfers between devices, local(): upper = lax.all_gather(shard, BOND, axis=0, tiled=True)  36.1 us
    ppermute x13, starting transfers between devices, move(): return lax.ppermute(x, NODE, pairs)  23.1 us
    dynamic_slice x3, local copies, waits for them, and re-layouts, halves(): return lax.dynamic_slice_in_dim(tensor, core * size, size, axis=axis)  21.2 us
    all_to_all x1, blocking collectives, local(): got = lax.all_to_all(send, NODE, 0, 0, tiled=True)  12.1 us
  transfers between devices with their start and end apart: 23, of which 3 were waited for; matrix products, arithmetic and copies ran while one was open for 60% of the time, Pallas kernels for 0%

commit v1 on v0

--- a/solution.py
+++ b/solution.py
@@ -2,10 +2,17 @@
 import jax.numpy as jnp
 from jax import lax
 from jax.sharding import Mesh, PartitionSpec as P
+from jax.lax import all_to_all, axis_size
 
 NODE = ("ylo", "zhi", "zlo")
 BOND = ("yhi", "x", "core")
 SLOT_OF = (4, 2, 5, 1, 6, 3, 7, 0)
+
+
+def check_area_here(block_here, at_axis):
+    vec_out = jnp.stack([block_here] * axis_size(BOND))
+    far_arr = all_to_all(vec_out, BOND, 0, 0)
+    return jnp.concatenate(far_arr, axis=at_axis)
 
 
 def ein(spec, a, b):
@@ -45,7 +52,7 @@
     send = jnp.stack([upper_nodes[s] for s in SLOT_OF])
     got = lax.all_to_all(send, NODE, 0, 0, tiled=True)
     shard = jnp.moveaxis(got, 0, 1).reshape(rows, width, width)
-    upper = lax.all_gather(shard, BOND, axis=0, tiled=True)
+    upper = check_area_here(shard, 0)
     mine = bottom_nodes[0]
     left_leaf = leaf_up[0, :, 0]
     right_leaf = leaf_up[0, :, 1]

time: 516 us -> 604 us (1.17)
  waiting for transfers between devices: 44.2 us -> 148 us
  blocking collectives: 61.9 us -> 9.22 us
  starting transfers between devices: 39.6 us -> 60.5 us
  matrix products: 236 us -> 246 us
    all_to_all x0 -> x3, waiting for transfers between devices: none -> 141 us  [the longest x1 113 us: check_area_here(): far_arr = all_to_all(vec_out, BOND, 0, 0)]
    all_to_all x2 -> x0, blocking collectives: 52.9 us -> none  [the longest x1 40.8 us: local(): both = lax.all_to_all(both, BOND, 0, 0, tiled=True)]
    all_gather x1 -> x0, waiting for transfers between devices: 36.1 us -> none  [local(): upper = lax.all_gather(shard, BOND, axis=0, tiled=True)]
    all_to_all x0 -> x3, starting transfers between devices: none -> 18.4 us  [the longest x1 7.76 us: local(): both = lax.all_to_all(both, BOND, 0, 0, tiled=True)]
    dot_general x36, matrix products: 236 us -> 246 us  [ein(): return jnp.einsum(spec, a, b, precision=lax.Precision.HIGHEST)]
    reshape x0 -> x1, local copies, waits for them, and re-layouts: none -> 9.43 us  [check_area_here(): return jnp.concatenate(far_arr, axis=at_axis)]
    all_gather x1 -> x0, local copies, waits for them, and re-layouts: 9.41 us -> none  [local(): upper = lax.all_gather(shard, BOND, axis=0, tiled=True)]
    all_to_all x0 -> x2, local copies, waits for them, and re-layouts: none -> 7.89 us  [the longest x1 7.86 us: check_area_here(): far_arr = all_to_all(vec_out, BOND, 0, 0)]
  transfers between devices with their start and end apart: 23 -> 25, of which waited for: 3 -> 5; matrix products, arithmetic and copies ran while one was open for 60% -> 54% of each run, Pallas kernels for 0% -> 0%
where the time goes in v1:
time: 604 us; the launch traced here: 596 us
  matrix products  246 us (41%)
  waiting for transfers between devices  148 us (25%)
  local copies, waits for them, and re-layouts  113 us (19%)
  starting transfers between devices  60.5 us (10%)
  between operations  15.2 us (3%)
  blocking collectives  9.22 us (2%)
    dot_general x36, matrix products, ein(): return jnp.einsum(spec, a, b, precision=lax.Precision.HIGHEST)  246 us
    all_to_all x1, waiting for transfers between devices, check_area_here(): far_arr = all_to_all(vec_out, BOND, 0, 0)  113 us
    dot_general x7, local copies, waits for them, and re-layouts, ein(): return jnp.einsum(spec, a, b, precision=lax.Precision.HIGHEST)  49.8 us
    all_to_all x1, waiting for transfers between devices, local(): both = lax.all_to_all(both, BOND, 0, 0, tiled=True)  23.3 us
    dynamic_slice x3, local copies, waits for them, and re-layouts, halves(): return lax.dynamic_slice_in_dim(tensor, core * size, size, axis=axis)  22.6 us
    ppermute x13, starting transfers between devices, move(): return lax.ppermute(x, NODE, pairs)  22 us
  transfers between devices with their start and end apart: 25, of which 5 were waited for; matrix products, arithmetic and copies ran while one was open for 54% of the time, Pallas kernels for 0%

profile of v1, /device:TPU:67, one launch (start us, length us, event | category | flops | bytes accessed | tf_op | source)
XLA Modules:
  0.0 596.0 jit_solution(7710201897402056958)
XLA Ops:
  16.3 7.8 %all-to-all-start.2 = ((f32[16,4,8,8,128]{4,3,2,1,0:T(8,128)}), f32[16,4,8,8,128]{4,3,2,1,0:T(8,128)S(1)}, u32[]{:S(2)}, u32[]{:S(2)}) async-start(f32[16,4,8,8,128]{4,3,2,1,0:T(8,128)} %copy_bitcast_fusion.1), calls=%async_computation.2 | async-start | bytes 4194304 | tf_op jit(solution)/shard_map/all_to_all | solution.py:63
  29.1 23.3 %all-to-all-done.2 = f32[16,4,8,8,128]{4,3,2,1,0:T(8,128)S(1)} async-done(((f32[16,4,8,8,128]{4,3,2,1,0:T(8,128)}), f32[16,4,8,8,128]{4,3,2,1,0:T(8,128)S(1)}, u32[]{:S(2)}, u32[]{:S(2)}) %all-to-all-start.2) | async-done | bytes 2097184 | tf_op jit(solution)/shard_map/all_to_all | solution.py:63
  63.9 7.0 %all-to-all-start.3 = ((f32[16,3,8,128]{3,2,1,0:T(8,128)}), f32[16,3,8,128]{3,2,1,0:T(8,128)S(1)}, u32[]{:S(2)}, u32[]{:S(2)}) async-start(f32[16,3,8,128]{3,2,1,0:T(8,128)} %bitcast.240), calls=%async_computation.3 | async-start | bytes 393216 | tf_op jit(solution)/shard_map/all_to_all | solution.py:68
  71.3 6.7 %all-to-all-done.3 = f32[16,3,8,128]{3,2,1,0:T(8,128)S(1)} async-done(((f32[16,3,8,128]{3,2,1,0:T(8,128)}), f32[16,3,8,128]{3,2,1,0:T(8,128)S(1)}, u32[]{:S(2)}, u32[]{:S(2)}) %all-to-all-start.3) | async-done | bytes 196640 | tf_op jit(solution)/shard_map/all_to_all | solution.py:68
  88.2 113.1 %all-to-all-done.1 = f32[16,8,128,128]{3,1,2,0:T(8,128)} async-done(((f32[16,8,128,128]{3,1,2,0:T(8,128)}), f32[16,8,128,128]{3,1,2,0:T(8,128)}, u32[]{:S(2)}, u32[]{:S(2)}) %all-to-all-start.1) | async-done | bytes 8388640 | tf_op jit(solution)/shard_map/all_to_all | solution.py:14
  209.0 7.9 %copy.208 = f32[16,8,128,128]{3,1,0,2:T(8,128)} copy(f32[16,8,128,128]{3,1,2,0:T(8,128)} %all-to-all-done.1) | data formatting | bytes 16777216 | tf_op jit(solution)/shard_map/all_to_all | solution.py:14
  221.8 8.4 %fusion.30 = f32[64,128,128]{2,1,0:T(8,128)S(1)} fusion(f32[64,128,128]{2,0,1:T(8,128)} %constant_dynamic-slice_fusion.1, f32[32,8,128]{2,1,0:T(8,128)S(1)} %all-to-all-done.4), kind=kOutput, calls=%fused_computation.31 | convolution fusion | flops 1610612736 | bytes 8454144 | tf_op jit(solution)/shard_map/pab,ac->pcb/dot_general | solution.py:19
  236.5 11.3 %convolution_bitcast_fusion.11 = f32[64,128]{1,0:T(8,128)S(1)} fusion(f32[64,128,128]{2,0,1:T(8,128)S(1)} %fusion.14, f32[16,8,128,128]{3,1,2,0:T(8,128)} %all-to-all-done.1), kind=kOutput, calls=%fused_computation.60 | convolution fusion | flops 1610612736 | bytes 12615680 | tf_op jit(solution)/shard_map/pcd,qcd->pq/dot_general | solution.py:19
  252.2 9.4 %copy.99 = f32[128,128,128]{1,0,2:T(8,128)} copy(f32[128,128,128]{2,0,1:T(8,128)} %bitcast.242) | data formatting | bytes 16777216 | tf_op jit(solution)/shard_map/reshape | solution.py:15
  273.6 10.7 %fusion.103 = f32[128,128,128]{1,0,2:T(8,128)S(1)} fusion(f32[128,128,128]{1,0,2:T(8,128)} %copy.99, f32[3,128,128]{2,1,0:T(8,128)S(1)} %copy-done, s32[]{:T(128)S(6)} %select_n.104), kind=kOutput, calls=%fused_computation.118 | convolution fusion | flops 3221225472 | bytes 16842756 | tf_op jit(solution)/shard_map/pq,qcd->pcd/dot_general | solution.py:19
  290.2 8.9 %constant_dynamic-slice_fusion = f32[128,128,64]{2,0,1:T(8,128)} fusion(f32[128,128,128]{2,0,1:T(8,128)} %bitcast.244, s32[]{:T(128)S(6)} %select_n.97), kind=kLoop, calls=%fused_computation.149 | loop fusion | bytes 8388612 | tf_op jit(solution)/shard_map/dynamic_slice | solution.py:41
  299.1 8.9 %copy.104 = f32[128,128,64]{1,0,2:T(8,128)} copy(f32[128,128,64]{2,0,1:T(8,128)} %constant_dynamic-slice_fusion) | data formatting | bytes 8388608 | tf_op jit(solution)/shard_map/dynamic_slice | solution.py:41
  309.8 12.0 %fusion.94 = f32[128,128,128]{2,0,1:T(8,128)} fusion(f32[64,128]{1,0:T(8,128)S(1)} %get-tuple-element.23, f32[64,128]{1,0:T(8,128)S(1)} %get-tuple-element.22, f32[16,8,128,128]{3,1,2,0:T(8,128)} %all-to-all-done.1), kind=kOutput, calls=%fused_computation.106 | convolution fusion | flops 3221241856 | bytes 16842752 | tf_op jit(solution)/shard_map/pq,qcd->pcd/dot_general | solution.py:19
  321.9 9.4 %copy.102 = f32[128,128,128]{1,0,2:T(8,128)} copy(f32[128,128,128]{2,0,1:T(8,128)} %fusion.94) | data formatting | bytes 16777216 | tf_op jit(solution)/shard_map/pq,qcd->pcd/dot_general | solution.py:19
  331.3 8.6 %fusion.33 = f32[64,128,128]{2,1,0:T(8,128)S(1)} fusion(f32[64,128,128]{2,0,1:T(8,128)} %constant_dynamic-slice_fusion.1, f32[2,64,128]{2,1,0:T(8,128)S(1)} %get-tuple-element.17, f32[2,64,128]{2,1,0:T(8,128)S(1)} %get-tuple-element.16), kind=kOutput, calls=%fused_computation.32 | convolution fusion | flops 1610629120 | bytes 8519680 | tf_op jit(solution)/shard_map/pab,ac->pcb/dot_general | solution.py:19
  346.3 11.3 %convolution_bitcast_fusion.10 = f32[64,128]{1,0:T(8,128)S(1)} fusion(f32[64,128,128]{2,0,1:T(8,128)S(1)} %fusion.12, f32[16,8,128,128]{3,1,2,0:T(8,128)} %all-to-all-done.1), kind=kOutput, calls=%fused_computation.59 | convolution fusion | flops 1610612736 | bytes 12615680 | tf_op jit(solution)/shard_map/pcd,qcd->pq/dot_general | solution.py:19
  381.0 11.0 %fusion.48 = f32[64,128]{1,0:T(8,128)S(1)} fusion(f32[128,128,128]{2,0,1:T(8,128)} %fusion.94, f32[128,128,64]{0,1,2:T(8,128)S(1)} %convolution_bitcast_fusion.2), kind=kOutput, calls=%fused_computation.48 | convolution fusion | flops 1610612736 | bytes 12615680 | tf_op jit(solution)/shard_map/pcb,pcd->bd/dot_general | solution.py:19
  403.1 8.3 %convolution_bitcast_fusion.8 = f32[64,128]{1,0:T(8,128)S(1)} fusion(f32[128,64,128]{0,1,2:T(8,128)} %copy.101, f32[128,128,128]{1,0,2:T(8,128)} %copy.102), kind=kOutput, calls=%fused_computation.57 | convolution fusion | flops 1610612736 | bytes 12615680 | tf_op jit(solution)/shard_map/pad,pcd->ac/dot_general | solution.py:19
  418.4 6.8 %fusion.4 = f32[64,128,128]{2,0,1:T(8,128)S(1)} fusion(f32[64,128,128]{2,1,0:T(8,128)S(1)} %fusion.36, f32[2,64,128]{2,1,0:T(8,128)S(1)} %get-tuple-element.14, f32[2,64,128]{2,1,0:T(8,128)S(1)} %get-tuple-element.15), kind=kOutput, calls=%fused_computation.5 | convolution fusion | flops 1610629120 | bytes 8519680 | tf_op jit(solution)/shard_map/pcb,bd->pcd/dot_general | solution.py:19
  425.5 11.1 %fusion.57 = f32[64,128]{1,0:T(8,128)S(1)} fusion(f32[64,128,128]{2,0,1:T(8,128)S(1)} %fusion.4, pred[]{:T(512)S(6)} %eq.9, f32[16,8,128,128]{3,1,2,0:T(8,128)} %all-to-all-done.1), kind=kOutput, calls=%fused_computation.52 | convolution fusion | flops 1610620928 | bytes 12615681 | tf_op jit(solution)/shard_map/pcd,qcd->pq/dot_general | solution.py:19
  437.3 11.6 %fusion.97 = f32[128,128,128]{2,0,1:T(8,128)} fusion(f32[64,128]{1,0:T(8,128)S(1)} %get-tuple-element.21, f32[64,128]{1,0:T(8,128)S(1)} %get-tuple-element.20, f32[16,8,128,128]{3,1,2,0:T(8,128)} %all-to-all-done.1), kind=kOutput, calls=%fused_computation.110 | convolution fusion | flops 3221241856 | bytes 16842752 | tf_op jit(solution)/shard_map/pq,qcd->pcd/dot_general | solution.py:19
  448.9 9.4 %copy.107 = f32[128,128,128]{1,0,2:T(8,128)} copy(f32[128,128,128]{2,0,1:T(8,128)} %fusion.97) | data formatting | bytes 16777216 | tf_op jit(solution)/shard_map/pq,qcd->pcd/dot_general | solution.py:19
  458.3 10.7 %fusion.51 = f32[64,128]{1,0:T(8,128)S(1)} fusion(f32[128,128,128]{2,0,1:T(8,128)} %fusion.97, f32[128,128,64]{0,1,2:T(8,128)} %convolution_bitcast_fusion.1), kind=kOutput, calls=%fused_computation.49 | convolution fusion | flops 1610612736 | bytes 12615680 | tf_op jit(solution)/shard_map/pcb,pcd->bd/dot_general | solution.py:19
  470.6 7.1 %convolution_bitcast_fusion.7 = f32[64,128]{1,0:T(8,128)S(1)} fusion(f32[128,64,128]{0,1,2:T(8,128)} %copy.106, f32[128,128,128]{1,0,2:T(8,128)S(1)} %copy-done.6), kind=kOutput, calls=%fused_computation.56 | convolution fusion | flops 1610612736 | bytes 12615680 | tf_op jit(solution)/shard_map/pad,pcd->ac/dot_general | solution.py:19
  496.6 10.5 %fusion.100 = f32[128,128,128]{2,0,1:T(8,128)S(1)} fusion(f32[64,128]{1,0:T(8,128)S(1)} %get-tuple-element.19, f32[64,128]{1,0:T(8,128)S(1)} %get-tuple-element.18, f32[16,8,128,128]{3,1,2,0:T(8,128)} %all-to-all-done.1), kind=kOutput, calls=%fused_computation.114 | convolution fusion | flops 3221241856 | bytes 16842752 | tf_op jit(solution)/shard_map/pq,qcd->pcd/dot_general | solution.py:19
  507.2 7.4 %fusion.54 = f32[64,128]{1,0:T(8,128)S(1)} fusion(f32[128,128,128]{2,0,1:T(8,128)S(1)} %fusion.100, f32[128,128,64]{0,1,2:T(8,128)S(1)} %copy-done.7), kind=kOutput, calls=%fused_computation.50 | convolution fusion | flops 1610612736 | bytes 12615680 | tf_op jit(solution)/shard_map/pcb,pcd->bd/dot_general | solution.py:19
  514.6 9.2 %collective-permute-start.14 = (f32[64,128]{1,0:T(8,128)S(1)}, f32[64,128]{1,0:T(8,128)S(1)}, u32[]{:S(2)}, u32[]{:S(2)}) collective-permute-start(f32[64,128]{1,0:T(8,128)S(1)} %fusion.54), channel_id=1, source_target_pairs={{0,16},{32,48},{64,80},{96,112},{1,17},{33,49},{65,81},{97,113},{2... | collective-permute-start | bytes 98312 | tf_op jit(solution)/shard_map/ppermute | solution.py:77
  523.8 9.4 %copy.112 = f32[128,128,128]{1,0,2:T(8,128)} copy(f32[128,128,128]{2,0,1:T(8,128)} %copy-done.2) | data formatting | bytes 16777216 | tf_op jit(solution)/shard_map/pq,qcd->pcd/dot_general | solution.py:19
  533.2 8.2 %fusion.59 = f32[1,64,128]{2,1,0:T(8,128)S(1)} fusion(f32[64,128]{1,0:T(8,128)S(1)} %collective-permute-done.14, f32[128,64,128]{0,1,2:T(8,128)} %copy.111, f32[128,128,128]{1,0,2:T(8,128)} %copy.112, pred[]{:T(512)S(6)} %eq.8), kind=kOutput, calls=%fused_computation.55 | convolution fusion | flops 1610620928 | bytes 12648449 | tf_op jit(solution)/shard_map/pad,pcd->ac/dot_general | solution.py:19
  541.4 9.2 %all-gather = f32[8,64,128]{2,1,0:T(8,128)S(1)} all-gather(f32[2,64,128]{2,1,0:T(8,128)S(1)} %pad_maximum_fusion.5), channel_id=2, replica_groups=mesh['ylo'=2,'zhi'=2,'zlo'=2,'yhi'=2,'x'=4,'core'=2] {'x'}, dimensions={0}, use_global_device_ids=true | all-gather | bytes 327680 | tf_op jit(solution)/shard_map/all_gather | solution.py:127
  565.3 9.4 %copy.124 = f32[128,128,128]{2,0,1:T(8,128)} copy(f32[128,128,128]{1,0,2:T(8,128)} %all-gather.3.cloned.1.call-done) | data formatting | bytes 16777216 | tf_op jit(solution)/shard_map/all_gather | solution.py:131
  574.7 6.8 %fusion.63 = f32[3,1,8,128]{3,2,0,1:T(8,128)S(1)} fusion(f32[128,128,128]{2,0,1:T(8,128)} %copy.124, f32[3,8,128,128]{3,1,2,0:T(8,128)S(1)} %fusion.112), kind=kOutput, calls=%fused_computation.62 | convolution fusion | flops 603979776 | bytes 9973760 | tf_op jit(solution)/shard_map/kbqc,qcd->kbd/dot_general | solution.py:19
  (159 shorter events, 170.1 us)
Async XLA Ops:
  7.2 266.4 %copy-start = (f32[3,128,128]{2,1,0:T(8,128)S(1)}, f32[3,128,128]{2,1,0:T(8,128)}, u32[]{:S(2)}) copy-start(f32[3,128,128]{2,1,0:T(8,128)} %param.9) | copy-start | bytes 589828
  16.3 36.1 %all-to-all-start.2 = ((f32[16,4,8,8,128]{4,3,2,1,0:T(8,128)}), f32[16,4,8,8,128]{4,3,2,1,0:T(8,128)S(1)}, u32[]{:S(2)}, u32[]{:S(2)}) async-start(f32[16,4,8,8,128]{4,3,2,1,0:T(8,128)} %copy_bitcast_fusion.1), calls=%async_computation.2 | async-start | bytes 4194304 | tf_op jit(solution)/shard_map/all_to_all | solution.py:63
  52.4 11.4 %all-to-all-start = ((f32[8,8,16,128]{3,2,1,0:T(8,128)}), f32[8,8,16,128]{3,2,1,0:T(8,128)S(1)}, u32[]{:S(2)}, u32[]{:S(2)}) async-start(f32[8,8,16,128]{3,2,1,0:T(8,128)} %slice_dynamic-update-slice_fusion), calls=%async_computation | async-start | bytes 1048576 | tf_op jit(solution)/shard_map/all_to_all | solution.py:53
  63.9 14.1 %all-to-all-start.3 = ((f32[16,3,8,128]{3,2,1,0:T(8,128)}), f32[16,3,8,128]{3,2,1,0:T(8,128)S(1)}, u32[]{:S(2)}, u32[]{:S(2)}) async-start(f32[16,3,8,128]{3,2,1,0:T(8,128)} %bitcast.240), calls=%async_computation.3 | async-start | bytes 393216 | tf_op jit(solution)/shard_map/all_to_all | solution.py:68
  82.1 119.2 %all-to-all-start.1 = ((f32[16,8,128,128]{3,1,2,0:T(8,128)}), f32[16,8,128,128]{3,1,2,0:T(8,128)}, u32[]{:S(2)}, u32[]{:S(2)}) async-start(f32[16,8,128,128]{3,1,2,0:T(8,128)} %stack.47), calls=%async_computation.1 | async-start | bytes 16777216 | tf_op jit(solution)/shard_map/all_to_all | solution.py:14
  202.0 19.8 %all-to-all-start.4 = ((f32[32,8,128]{2,1,0:T(8,128)}), f32[32,8,128]{2,1,0:T(8,128)S(1)}, u32[]{:S(2)}, u32[]{:S(2)}) async-start(f32[32,8,128]{2,1,0:T(8,128)} %bitcast.23), calls=%async_computation.4 | async-start | bytes 262144 | tf_op jit(solution)/shard_map/all_to_all | solution.py:73
  208.5 352.3 %all-gather.3.cloned.1.call-start = ((), (), s32[]{:S(2)}) async-start(), calls=%async_computation.5 | async-start | bytes 8912896 | tf_op jit(solution)/shard_map/all_gather | solution.py:131
  247.8 61.2 %collective-permute-start = (f32[64,128]{1,0:T(8,128)S(1)}, f32[64,128]{1,0:T(8,128)S(1)}, u32[]{:S(2)}, u32[]{:S(2)}) collective-permute-start(f32[64,128]{1,0:T(8,128)S(1)} %convolution_bitcast_fusion.11), channel_id=1, source_target_pairs={{0,16},{64,80},{1,17},{65,81},{2,18},{66,82},{3,19},{67,83},{4,20}... | collective-permute-start | bytes 98312 | tf_op jit(solution)/shard_map/ppermute | solution.py:77
  248.5 60.5 %collective-permute-start.1 = (f32[64,128]{1,0:T(8,128)S(1)}, f32[64,128]{1,0:T(8,128)S(1)}, u32[]{:S(2)}, u32[]{:S(2)}) collective-permute-start(f32[64,128]{1,0:T(8,128)S(1)} %convolution_bitcast_fusion.11), channel_id=1, source_target_pairs={{32,16},{96,80},{33,17},{97,81},{34,18},{98,82},{35,19},{99,83},{3... | collective-permute-start | bytes 98312 | tf_op jit(solution)/shard_map/ppermute | solution.py:77
  289.6 18.4 %collective-permute-start.6 = (f32[64,128]{1,0:T(8,128)S(1)}, f32[64,128]{1,0:T(8,128)S(1)}, u32[]{:S(2)}, u32[]{:S(2)}) collective-permute-start(f32[64,128]{1,0:T(8,128)S(1)} %convolution_bitcast_fusion.9), channel_id=1, source_target_pairs={{112,48},{113,49},{114,50},{115,51},{116,52},{117,53},{118,54},{11... | collective-permute-start | bytes 98312 | tf_op jit(solution)/shard_map/ppermute | solution.py:77
  308.0 1.8 collective-permute-start.7
  309.0 22.3 %collective-permute-start.2 = (f32[2,64,128]{2,1,0:T(8,128)S(1)}, f32[2,64,128]{2,1,0:T(8,128)S(1)}, u32[]{:S(2)}, u32[]{:S(2)}) collective-permute-start(f32[2,64,128]{2,1,0:T(8,128)S(1)} %pad_maximum_fusion.3), channel_id=1, source_target_pairs={{0,1},{1,0},{2,3},{3,2},{4,5},{5,4},{6,7},{7,6},{8,9},{9,8},{10,11... | collective-permute-start | bytes 196616 | tf_op jit(solution)/shard_map/ppermute | solution.py:27
  339.9 25.1 %slice-start = ((s8[8388608]{0:T(1024)(128)(4,1)}), s8[4194304]{0:T(1024)(128)(4,1)S(1)}, s32[]{:S(2)}) async-start(s8[8388608]{0:T(1024)(128)(4,1)} %bitcast.245), calls=%async_computation.6 | async-start | bytes 8388608
  346.3 18.8 %slice-start.1 = ((s8[8388608]{0:T(1024)(128)(4,1)}), s8[4194304]{0:T(1024)(128)(4,1)S(1)}, s32[]{:S(2)}) async-start(s8[8388608]{0:T(1024)(128)(4,1)} %bitcast.245), calls=%async_computation.7 | async-start | bytes 8388608
  357.6 7.0 %collective-permute-start.3 = (f32[64,128]{1,0:T(8,128)S(1)}, f32[64,128]{1,0:T(8,128)S(1)}, u32[]{:S(2)}, u32[]{:S(2)}) collective-permute-start(f32[64,128]{1,0:T(8,128)S(1)} %convolution_bitcast_fusion.10), channel_id=1, source_target_pairs={{16,48},{17,49},{18,50},{19,51},{20,52},{21,53},{22,54},{23,55},{2... | collective-permute-start | bytes 98312 | tf_op jit(solution)/shard_map/ppermute | solution.py:77
  358.2 6.3 %collective-permute-start.4 = (f32[64,128]{1,0:T(8,128)S(1)}, f32[64,128]{1,0:T(8,128)S(1)}, u32[]{:S(2)}, u32[]{:S(2)}) collective-permute-start(f32[64,128]{1,0:T(8,128)S(1)} %convolution_bitcast_fusion.10), channel_id=1, source_target_pairs={{80,48},{81,49},{82,50},{83,51},{84,52},{85,53},{86,54},{87,55},{8... | collective-permute-start | bytes 98312 | tf_op jit(solution)/shard_map/ppermute | solution.py:77
  364.6 10.8 %collective-permute-start.5 = (f32[2,64,128]{2,1,0:T(8,128)S(1)}, f32[2,64,128]{2,1,0:T(8,128)S(1)}, u32[]{:S(2)}, u32[]{:S(2)}) collective-permute-start(f32[2,64,128]{2,1,0:T(8,128)S(1)} %pad_maximum_fusion.4), channel_id=1, source_target_pairs={{0,1},{1,0},{2,3},{3,2},{4,5},{5,4},{6,7},{7,6},{8,9},{9,8},{10,11... | collective-permute-start | bytes 196616 | tf_op jit(solution)/shard_map/ppermute | solution.py:27
  375.4 17.3 %slice-start.2 = ((s8[8388608]{0:T(1024)(128)(4,1)}), s8[4194304]{0:T(1024)(128)(4,1)S(1)}, s32[]{:S(2)}) async-start(s8[8388608]{0:T(1024)(128)(4,1)} %bitcast.248), calls=%async_computation.8 | async-start | bytes 8388608
  392.0 33.2 %collective-permute-start.9 = (f32[64,128]{1,0:T(8,128)S(1)}, f32[64,128]{1,0:T(8,128)S(1)}, u32[]{:S(2)}, u32[]{:S(2)}) collective-permute-start(f32[64,128]{1,0:T(8,128)S(1)} %fusion.48), channel_id=1, source_target_pairs={{48,80},{49,81},{50,82},{51,83},{52,84},{53,85},{54,86},{55,87},{5... | collective-permute-start | bytes 98312 | tf_op jit(solution)/shard_map/ppermute | solution.py:77
  411.4 13.8 %collective-permute-start.8 = (f32[64,128]{1,0:T(8,128)S(1)}, f32[64,128]{1,0:T(8,128)S(1)}, u32[]{:S(2)}, u32[]{:S(2)}) collective-permute-start(f32[64,128]{1,0:T(8,128)S(1)} %convolution_bitcast_fusion.8), channel_id=1, source_target_pairs={{48,16},{49,17},{50,18},{51,19},{52,20},{53,21},{54,22},{55,23},{5... | collective-permute-start | bytes 98312 | tf_op jit(solution)/shard_map/ppermute | solution.py:77
  425.2 12.1 %collective-permute-start.10 = (f32[64,128]{1,0:T(8,128)S(1)}, f32[64,128]{1,0:T(8,128)S(1)}, u32[]{:S(2)}, u32[]{:S(2)}) collective-permute-start(f32[64,128]{1,0:T(8,128)S(1)} %add.49), channel_id=1, source_target_pairs={{0,1},{1,0},{2,3},{3,2},{4,5},{5,4},{6,7},{7,6},{8,9},{9,8},{10,11... | collective-permute-start | bytes 98312 | tf_op jit(solution)/shard_map/ppermute | solution.py:27
  436.6 47.1 %collective-permute-start.15 = (f32[64,128]{1,0:T(8,128)S(1)}, f32[64,128]{1,0:T(8,128)S(1)}, u32[]{:S(2)}, u32[]{:S(2)}) collective-permute-start(f32[64,128]{1,0:T(8,128)S(1)} %fusion.57), channel_id=1, source_target_pairs={{48,112},{49,113},{50,114},{51,115},{52,116},{53,117},{54,118},{55... | collective-permute-start | bytes 98312 | tf_op jit(solution)/shard_map/ppermute | solution.py:77
  458.3 26.6 %slice-start.4 = ((s8[8388608]{0:T(1024)(128)(4,1)}), s8[4194304]{0:T(1024)(128)(4,1)S(1)}, s32[]{:S(2)}) async-start(s8[8388608]{0:T(1024)(128)(4,1)} %bitcast.251), calls=%async_computation.10 | async-start | bytes 8388608
  469.0 15.9 %slice-start.5 = ((s8[8388608]{0:T(1024)(128)(4,1)}), s8[4194304]{0:T(1024)(128)(4,1)S(1)}, s32[]{:S(2)}) async-start(s8[8388608]{0:T(1024)(128)(4,1)} %bitcast.251), calls=%async_computation.11 | async-start | bytes 8388608
  469.0 15.4 %collective-permute-start.12 = (f32[64,128]{1,0:T(8,128)S(1)}, f32[64,128]{1,0:T(8,128)S(1)}, u32[]{:S(2)}, u32[]{:S(2)}) collective-permute-start(f32[64,128]{1,0:T(8,128)S(1)} %fusion.51), channel_id=1, source_target_pairs={{16,32},{80,96},{17,33},{81,97},{18,34},{82,98},{19,35},{83,99},{2... | collective-permute-start | bytes 98312 | tf_op jit(solution)/shard_map/ppermute | solution.py:77
  477.7 6.7 %collective-permute-start.11 = (f32[64,128]{1,0:T(8,128)S(1)}, f32[64,128]{1,0:T(8,128)S(1)}, u32[]{:S(2)}, u32[]{:S(2)}) collective-permute-start(f32[64,128]{1,0:T(8,128)S(1)} %convolution_bitcast_fusion.7), channel_id=1, source_target_pairs={{16,0},{80,64},{17,1},{81,65},{18,2},{82,66},{19,3},{83,67},{20,4}... | collective-permute-start | bytes 98312 | tf_op jit(solution)/shard_map/ppermute | solution.py:77
  483.8 11.5 %collective-permute-start.16 = (f32[64,128]{1,0:T(8,128)S(1)}, f32[64,128]{1,0:T(8,128)S(1)}, u32[]{:S(2)}, u32[]{:S(2)}) collective-permute-start(f32[64,128]{1,0:T(8,128)S(1)} %add.51), channel_id=1, source_target_pairs={{48,16},{112,80},{49,17},{113,81},{50,18},{114,82},{51,19},{115,83... | collective-permute-start | bytes 98312 | tf_op jit(solution)/shard_map/ppermute | solution.py:77
  484.5 12.1 %collective-permute-start.13 = (f32[64,128]{1,0:T(8,128)S(1)}, f32[64,128]{1,0:T(8,128)S(1)}, u32[]{:S(2)}, u32[]{:S(2)}) collective-permute-start(f32[64,128]{1,0:T(8,128)S(1)} %add.50), channel_id=1, source_target_pairs={{0,1},{1,0},{2,3},{3,2},{4,5},{5,4},{6,7},{7,6},{8,9},{9,8},{10,11... | collective-permute-start | bytes 98312 | tf_op jit(solution)/shard_map/ppermute | solution.py:27
  495.3 28.5 %collective-permute-start.17 = (f32[64,128]{1,0:T(8,128)S(1)}, f32[64,128]{1,0:T(8,128)S(1)}, u32[]{:S(2)}, u32[]{:S(2)}) collective-permute-start(f32[64,128]{1,0:T(8,128)S(1)} %add.52), channel_id=1, source_target_pairs={{48,32},{16,0},{112,96},{80,64},{49,33},{17,1},{113,97},{81,65},{5... | collective-permute-start | bytes 98312 | tf_op jit(solution)/shard_map/ppermute | solution.py:77
  514.6 18.6 %collective-permute-start.14 = (f32[64,128]{1,0:T(8,128)S(1)}, f32[64,128]{1,0:T(8,128)S(1)}, u32[]{:S(2)}, u32[]{:S(2)}) collective-permute-start(f32[64,128]{1,0:T(8,128)S(1)} %fusion.54), channel_id=1, source_target_pairs={{0,16},{32,48},{64,80},{96,112},{1,17},{33,49},{65,81},{97,113},{2... | collective-permute-start | bytes 98312 | tf_op jit(solution)/shard_map/ppermute | solution.py:77
  533.2 21.3 %copy-start.13 = (f32[1,3,2,128,128]{4,3,2,1,0:T(8,128)S(1)}, f32[1,3,2,128,128]{4,3,2,1,0:T(8,128)}, u32[]{:S(2)}) copy-start(f32[1,3,2,128,128]{4,3,2,1,0:T(8,128)} %param.7) | copy-start | bytes 1179652
  550.7 5.8 collective-permute-start.18
  (16 other events, 135.9 us)
Sparse Core Ops, SparseCore 0:
  217.0 80.1 all-gather.2
